TPU v7x, 32 devices: a whole 2x2x4 slice. The times are simulated.
32 devices in a mesh: ens: 4 (over x, core), space: 8 (over z, y).
Axes of the slice: x: 2, y: 2, z: 4, core: 2. Of those that a mesh axis runs over, the one named last changes fastest.
Arguments:
- latents: bfloat16 [8, 32, 256, 256], P('ens', None, 'space'), may hold values from -6 to 6
- targets: bfloat16 [32, 256, 256], P(None, 'space'), may hold values from -6 to 6
- kernel: bfloat16 [3, 3, 256, 256], replicated, may hold values from -0.125 to 0.125
Outputs:
- loss: float32 [], replicated
- grad_input: bfloat16 [8, 32, 256, 256], P('ens', None, 'space')
- grad_kernel: float32 [3, 3, 256, 256], replicated
All inputs are finite; a program needn't handle non-finite values.
Results may differ from a plain program's by a relative error of at most 0.0047.
Values may be sent and summed in bfloat16 or wider, within the bound.
A program may use at most 64 MiB of HBM per device.

v0:
```python
import jax
import jax.numpy as jnp
from jax import lax
from jax.sharding import PartitionSpec as P

smoothing = 0.1


def padded_2(block, sides, width):
    for axis, dim in sides:
        count = lax.axis_size(axis)
        forward = [(i, i + 1) for i in range(count - 1)]
        forward.append((count - 1, 0))
        backward = [(target, source) for source, target in forward]
        low = lax.ppermute(
            lax.slice_in_dim(block, block.shape[dim] - width, None, axis=dim), axis, forward
        )
        high = lax.ppermute(lax.slice_in_dim(block, 0, width, axis=dim), axis, backward)
        block = jnp.concatenate([low, block, high], axis=dim)
    return block


def lat_pad(field):
    return jnp.pad(field, ((0, 0), (1, 1), (0, 0), (0, 0)))


def conv_forward(padded, kernel, rows, cols):
    chans = padded.shape[3]
    total = None
    for row_off in range(3):
        for col_off in range(3):
            window = padded[:, row_off : row_off + rows, col_off : col_off + cols, :].reshape(
                -1, chans
            )
            term = jnp.dot(window, kernel[row_off, col_off], preferred_element_type=jnp.float32)
            total = term if total is None else total + term
    return total.reshape(padded.shape[0], rows, cols, -1)


def conv_adjoint(padded, kernel, rows, cols):
    chans = padded.shape[3]
    total = None
    for row_off in range(3):
        for col_off in range(3):
            window = padded[
                :, 2 - row_off : 2 - row_off + rows, 2 - col_off : 2 - col_off + cols, :
            ].reshape(-1, chans)
            term = lax.dot_general(
                window,
                kernel[row_off, col_off],
                (((1,), (1,)), ((), ())),
                preferred_element_type=jnp.float32,
            )
            total = term if total is None else total + term
    return total.reshape(padded.shape[0], rows, cols, -1)


def kernel_terms(padded, slopes, rows, cols):
    chans = padded.shape[3]
    flat_slopes = slopes.reshape(-1, slopes.shape[3])
    blocks = []
    for row_off in range(3):
        for col_off in range(3):
            window = padded[:, row_off : row_off + rows, col_off : col_off + cols, :].reshape(
                -1, chans
            )
            blocks.append(
                lax.dot_general(
                    window,
                    flat_slopes,
                    (((0,), (0,)), ((), ())),
                    preferred_element_type=jnp.float32,
                )
            )
    return jnp.stack(blocks).reshape(3, 3, chans, -1)


def local(latents, targets, kernel):
    members_dev, rows, cols, chans = latents.shape
    members = members_dev * lax.axis_size("ens")
    longitude = cols * lax.axis_size("space")
    rimmed = padded_2(latents, (("space", 2),), 1)
    padded = lat_pad(rimmed)
    fields = conv_forward(padded, kernel, rows, cols)
    offset = fields - targets.astype(jnp.float32)[None]
    spread = jnp.sqrt(offset * offset + smoothing * smoothing)
    own_total = jnp.sum(spread)
    own_slope = offset / spread
    block = lax.all_to_all(fields, "ens", split_axis=1, concat_axis=0, tiled=True)
    gap = block[:, None] - block[None]
    width = jnp.sqrt(gap * gap + smoothing * smoothing)
    slope = jnp.sum(gap / width, axis=1)
    returned = lax.all_to_all(slope, "ens", split_axis=0, concat_axis=1, tiled=True)
    part_total = jnp.sum(width, axis=(0, 1))[None] - block.shape[0] * smoothing
    pair_total = jnp.sum(part_total)
    slopes = (own_slope / members - returned / (members * (members - 1))).astype(jnp.bfloat16)
    cell_sum = own_total / members - pair_total / (2 * members * (members - 1))
    slope_rimmed = padded_2(slopes, (("space", 2),), 1)
    grad_input = conv_adjoint(lat_pad(slope_rimmed), kernel, rows, cols).astype(jnp.bfloat16)
    partial_kernel = kernel_terms(padded, slopes, rows, cols) / (members * rows * longitude)
    grad_kernel, loss_total = lax.psum((partial_kernel, cell_sum), ("ens", "space"))
    loss = loss_total / (rows * longitude * chans)
    return (loss, grad_input, grad_kernel)


def solution(mesh):
    in_specs = (P("ens", None, "space", None), P(None, "space", None), P())
    out_specs = (P(), P("ens", None, "space", None), P())
    return jax.shard_map(local, mesh=mesh, in_specs=in_specs, out_specs=out_specs, check_vma=False)
```

profile of v0, /device:TPU:0, one launch (start us, length us, event | category | flops | bytes accessed | tf_op | source)
XLA Modules:
  0.0 301.2 jit_solution(1788002785526001829)
XLA Ops:
  7.2 1.2 fusion.72
  8.4 3.0 %collective-permute-start = (bf16[2,32,1,256]{3,2,1,0:T(2,128)(2,1)S(1)}, bf16[2,32,1,256]{3,2,1,0:T(2,128)(2,1)S(1)}, u32[]{:S(2)}, u32[]{:S(2)}) collective-permute-start(bf16[2,32,1,256]{3,2,1,0:T(2,128)(2,1)S(1)} %get-tuple-element.25), channel_id=1, source_target_pairs={{0,1},{1,2},{2,3},{3,4},{4,5},{5,6},{6,7},{7,0},{8,9},{9,10},{10,1... | collective-permute-start | bytes 98312 | tf_op jit(solution)/shard_map/ppermute | solution.py:15
  11.4 3.1 %collective-permute-start.1 = (bf16[2,32,1,256]{3,2,1,0:T(2,128)(2,1)S(1)}, bf16[2,32,1,256]{3,2,1,0:T(2,128)(2,1)S(1)}, u32[]{:S(2)}, u32[]{:S(2)}) collective-permute-start(bf16[2,32,1,256]{3,2,1,0:T(2,128)(2,1)S(1)} %get-tuple-element.26), channel_id=1, source_target_pairs={{1,0},{2,1},{3,2},{4,3},{5,4},{6,5},{7,6},{0,7},{9,8},{10,9},{11,1... | collective-permute-start | bytes 98312 | tf_op jit(solution)/shard_map/ppermute | solution.py:18
  14.5 1.7 fusion.33
  16.2 0.6 collective-permute-done
  16.8 0.3 collective-permute-done.1
  17.1 0.8 select_maximum_fusion.2
  17.9 1.0 fusion.70
  18.9 0.3 copy-done.9
  19.2 0.4 fusion.27
  19.6 0.4 fusion.43
  20.1 0.4 convolution_add_fusion.11
  20.5 0.4 convolution_add_fusion.10
  20.9 1.2 pad_maximum_fusion.2
  22.2 0.4 fusion.8
  22.6 0.5 copy-done.5
  23.1 0.4 copy-done.3
  23.5 0.4 fusion.7
  23.9 0.4 convolution_add_fusion.7
  24.3 0.4 convolution_add_fusion.6
  24.9 28.3 %all_to_all.24 = f32[2,32,32,256]{3,2,0,1:T(8,128)S(1)} all-to-all(f32[2,32,32,256]{3,2,0,1:T(8,128)S(1)} %copy.19), channel_id=1, replica_groups=mesh['ens'=4,'space'=8] {'ens'}, dimensions={1} | all-to-all | bytes 4194304 | tf_op jit(solution)/shard_map/all_to_all | solution.py:89
  53.2 0.2 copy.21
  53.4 9.9 %fusion.3 = (f32[8,8,32,256]{3,2,1,0:T(8,128)}, f32[8,32,256]{2,1,0:T(8,128)}) fusion(f32[8,8,32,256]{3,2,1,0:T(8,128)S(1)} %bitcast.208), kind=kLoop, calls=%fused_computation.5 | loop fusion | flops 24576000 | bytes 4456448 | tf_op jit(solution)/shard_map/reduce_sum | solution.py:92
  63.4 4.4 %all-to-all-start.1 = ((f32[8,8,32,256]{3,2,1,0:T(8,128)}), f32[8,8,32,256]{3,2,1,0:T(8,128)}, u32[]{:S(2)}, u32[]{:S(2)}) async-start(f32[8,8,32,256]{3,2,1,0:T(8,128)} %get-tuple-element.3), calls=%async_computation.1 | async-start | bytes 4194304 | tf_op jit(solution)/shard_map/all_to_all | solution.py:93
  67.8 0.2 all-reduce.4.cloned.1.call-start
  68.1 2.1 convert_element_type.18
  70.2 1.6 add_reduce_fusion
  72.5 21.1 %all-to-all-done.1 = f32[8,8,32,256]{3,2,1,0:T(8,128)} async-done(((f32[8,8,32,256]{3,2,1,0:T(8,128)}), f32[8,8,32,256]{3,2,1,0:T(8,128)}, u32[]{:S(2)}, u32[]{:S(2)}) %all-to-all-start.1) | async-done | bytes 2097184 | tf_op jit(solution)/shard_map/all_to_all | solution.py:93
  93.6 1.8 broadcast_multiply_fusion.1
  95.4 0.2 copy.22
  95.7 1.0 copy-done.7
  96.6 2.8 fusion.10
  99.4 2.3 subtract_convert_fusion
  101.6 0.8 fusion.71
  102.4 0.5 fusion.20
  102.9 1.1 collective-permute-start.2
  103.9 3.7 %collective-permute-start.3 = (bf16[2,32,1,256]{3,2,1,0:T(2,128)(2,1)}, bf16[2,32,1,256]{3,2,1,0:T(2,128)(2,1)}, u32[]{:S(2)}, u32[]{:S(2)}) collective-permute-start(bf16[2,32,1,256]{3,2,1,0:T(2,128)(2,1)} %get-tuple-element.22), channel_id=1, source_target_pairs={{1,0},{2,1},{3,2},{4,3},{5,4},{6,5},{7,6},{0,7},{9,8},{10,9},{11,1... | collective-permute-start | bytes 98312 | tf_op jit(solution)/shard_map/ppermute | solution.py:18
  107.6 0.5 fusion.19
  108.2 0.5 fusion.18
  108.6 0.7 copy-done.6
  109.4 0.5 fusion.17
  109.9 0.5 fusion.16
  110.4 0.3 copy-done.4
  110.7 0.5 fusion.15
  111.2 0.5 fusion.14
  111.7 0.5 fusion.13
  112.1 0.5 fusion.12
  112.7 1.6 broadcast_multiply_fusion
  114.9 0.2 copy-done.11
  115.1 1.8 fusion.31
  116.8 37.0 %psum.14 = f32[]{:T(128)} all-reduce(f32[]{:T(128)S(6)} %sub.50), channel_id=1, replica_groups=mesh['ens'=4,'space'=8] {'ens','space'}, use_global_device_ids=true, to_apply=%region_3.4 | all-reduce | flops 1 | bytes 8 | tf_op jit(solution)/shard_map/psum | solution.py:101
  154.6 1.7 select_maximum_fusion
  156.3 1.0 fusion.69
  157.2 0.5 fusion.41
  157.7 0.5 convolution_add_fusion.5
  158.2 0.5 convolution_add_fusion.4
  158.7 2.1 pad_maximum_fusion
  160.8 0.5 fusion.6
  161.2 0.5 fusion.25
  161.7 0.5 fusion.5
  162.2 0.5 convolution_add_fusion.1
  162.7 1.4 fusion.9
  164.1 125.8 %all-reduce.4.cloned.1.call-done = f32[3,3,256,256]{3,2,1,0:T(8,128)} async-done(((f32[3,3,256,256]{3,2,1,0:T(8,128)}), f32[3,3,256,256]{3,2,1,0:T(8,128)}) %all-reduce.4.cloned.1.call-update) | async-done | bytes 2359312 | tf_op jit(solution)/shard_map/psum | solution.py:101
  290.0 3.2 %copy.45 = f32[3,3,256,256]{3,2,1,0:T(8,128)} copy(f32[3,3,256,256]{3,2,1,0:T(8,128)} %all-reduce.4.cloned.1.call-done) | data formatting | bytes 4718592
  (21 shorter events, 0.2 us)
Async XLA Ops:
  7.2 9.9 %copy-start.1 = (bf16[2,32,32,256]{3,2,1,0:T(8,128)(2,1)S(1)}, bf16[2,32,32,256]{3,2,1,0:T(8,128)(2,1)}, u32[]{:S(2)}) copy-start(bf16[2,32,32,256]{3,2,1,0:T(8,128)(2,1)} %param.3) | copy-start | bytes 3145732
  8.4 8.4 %collective-permute-start = (bf16[2,32,1,256]{3,2,1,0:T(2,128)(2,1)S(1)}, bf16[2,32,1,256]{3,2,1,0:T(2,128)(2,1)S(1)}, u32[]{:S(2)}, u32[]{:S(2)}) collective-permute-start(bf16[2,32,1,256]{3,2,1,0:T(2,128)(2,1)S(1)} %get-tuple-element.25), channel_id=1, source_target_pairs={{0,1},{1,2},{2,3},{3,4},{4,5},{5,6},{6,7},{7,0},{8,9},{9,10},{10,1... | collective-permute-start | bytes 98312 | tf_op jit(solution)/shard_map/ppermute | solution.py:15
  11.4 5.7 %collective-permute-start.1 = (bf16[2,32,1,256]{3,2,1,0:T(2,128)(2,1)S(1)}, bf16[2,32,1,256]{3,2,1,0:T(2,128)(2,1)S(1)}, u32[]{:S(2)}, u32[]{:S(2)}) collective-permute-start(bf16[2,32,1,256]{3,2,1,0:T(2,128)(2,1)S(1)} %get-tuple-element.26), channel_id=1, source_target_pairs={{1,0},{2,1},{3,2},{4,3},{5,4},{6,5},{7,6},{0,7},{9,8},{10,9},{11,1... | collective-permute-start | bytes 98312 | tf_op jit(solution)/shard_map/ppermute | solution.py:18
  17.9 1.3 copy-start.9
  22.1 1.0 copy-start.5
  22.2 1.3 copy-start.3
  24.8 70.9 %copy-start = (f32[2048,256]{1,0:T(8,128)}, f32[2048,256]{1,0:T(8,128)S(1)}, u32[]{:S(2)}) copy-start(f32[2048,256]{1,0:T(8,128)S(1)} %convolution_add_fusion.6) | copy-start | bytes 6291460
  63.4 30.2 %all-to-all-start.1 = ((f32[8,8,32,256]{3,2,1,0:T(8,128)}), f32[8,8,32,256]{3,2,1,0:T(8,128)}, u32[]{:S(2)}, u32[]{:S(2)}) async-start(f32[8,8,32,256]{3,2,1,0:T(8,128)} %get-tuple-element.3), calls=%async_computation.1 | async-start | bytes 4194304 | tf_op jit(solution)/shard_map/all_to_all | solution.py:93
  67.8 222.1 %all-reduce.4.cloned.1.call-start = ((), (), s32[]{:S(2)}) async-start(), calls=%async_computation.2 | async-start | bytes 4718592 | tf_op jit(solution)/shard_map/psum | solution.py:101
  95.4 1.2 copy-start.7
  102.9 51.7 %collective-permute-start.2 = (bf16[2,32,1,256]{3,2,1,0:T(2,128)(2,1)}, bf16[2,32,1,256]{3,2,1,0:T(2,128)(2,1)S(1)}, u32[]{:S(2)}, u32[]{:S(2)}) collective-permute-start(bf16[2,32,1,256]{3,2,1,0:T(2,128)(2,1)} %get-tuple-element.21), channel_id=1, source_target_pairs={{0,1},{1,2},{2,3},{3,4},{4,5},{5,6},{6,7},{7,0},{8,9},{9,10},{10,1... | collective-permute-start | bytes 98312 | tf_op jit(solution)/shard_map/ppermute | solution.py:15
  103.9 50.6 %collective-permute-start.3 = (bf16[2,32,1,256]{3,2,1,0:T(2,128)(2,1)}, bf16[2,32,1,256]{3,2,1,0:T(2,128)(2,1)}, u32[]{:S(2)}, u32[]{:S(2)}) collective-permute-start(bf16[2,32,1,256]{3,2,1,0:T(2,128)(2,1)} %get-tuple-element.22), channel_id=1, source_target_pairs={{1,0},{2,1},{3,2},{4,3},{5,4},{6,5},{7,6},{0,7},{9,8},{10,9},{11,1... | collective-permute-start | bytes 98312 | tf_op jit(solution)/shard_map/ppermute | solution.py:18
  108.1 1.2 copy-start.6
  108.2 1.7 copy-start.2
  109.4 1.3 copy-start.4
  112.6 2.3 copy-start.10
  112.6 2.4 copy-start.11
  158.7 2.1 copy-start.8
Sparse Core Ops, SparseCore 0:
  154.0 135.8 all-reduce.3
where the time goes:
time: 302 us; the launch traced here: 301 us
  waiting for transfers between devices  148 us (49%)
  blocking collectives  65.3 us (22%)
  other arithmetic  27.9 us (9%)
  between operations  17.5 us (6%)
  matrix products  16 us (5%)
  starting transfers between devices  15.6 us (5%)
  local copies, waits for them, and re-layouts  11.1 us (4%)
    psum x1, waiting for transfers between devices, local(): lax.psum((partial_kernel, cell_sum), ('ens', 'space'))  126 us
    psum x1, blocking collectives, local(): lax.psum((partial_kernel, cell_sum), ('ens', 'space'))  37 us
    all_to_all x1, blocking collectives, local(): lax.all_to_all(fields, 'ens', split_axis=1, concat_axis=0, tiled=True)  28.3 us
    all_to_all x1, waiting for transfers between devices, local(): lax.all_to_all(slope, 'ens', split_axis=0, concat_axis=1, tiled=True)  21.1 us
    reduce_sum x1, other arithmetic, local(): slope = jnp.sum(gap / width, axis=1)  9.94 us
    ppermute x2, starting transfers between devices, padded_2(): lax.ppermute(lax.slice_in_dim(block, 0, width, axis=dim), axis, backward)  6.82 us
    unnamed x25, local copies, waits for them, and re-layouts  6.52 us
    dot_general x9, matrix products, conv_adjoint(): lax.dot_general(window, kernel[row_off, col_off], (((1,), (1,)), ((), ())...  6.51 us
  transfers between devices with their start and end apart: 6, of which 4 were waited for; matrix products, arithmetic and copies ran while one was open for 7% of the time, Pallas kernels for 0%

commit v1 on v0

--- a/solution.py
+++ b/solution.py
@@ -1,9 +1,18 @@
+import functools
 import jax
 import jax.numpy as jnp
 from jax import lax
 from jax.sharding import PartitionSpec as P
 
 smoothing = 0.1
+
+
+def supply_steps_all(slab_in, peer_axis, shard_axis):
+    near = lax.psum(lax.psum(slab_in, axis_name=peer_axis), axis_name=shard_axis)
+    return near
+
+
+_read_shards = functools.partial(supply_steps_all, peer_axis="space", shard_axis="ens")
 
 
 def padded_2(block, sides, width):
@@ -98,7 +107,7 @@
     slope_rimmed = padded_2(slopes, (("space", 2),), 1)
     grad_input = conv_adjoint(lat_pad(slope_rimmed), kernel, rows, cols).astype(jnp.bfloat16)
     partial_kernel = kernel_terms(padded, slopes, rows, cols) / (members * rows * longitude)
-    grad_kernel, loss_total = lax.psum((partial_kernel, cell_sum), ("ens", "space"))
+    grad_kernel, loss_total = _read_shards((partial_kernel, cell_sum))
     loss = loss_total / (rows * longitude * chans)
     return (loss, grad_input, grad_kernel)
 

time: 302 us -> 318 us (1.053)
  matrix products: 16 us -> 27.5 us
  blocking collectives: 65.3 us -> 57.3 us
  waiting for transfers between devices: 148 us -> 156 us
    psum x1 -> x2, waiting for transfers between devices: 126 us -> 134 us  [the longest x1 82.6 us: supply_steps_all(): lax.psum(slab_in, axis_name=peer_axis)]
    psum x1 -> x2, blocking collectives: 37 us -> 29 us  [the longest x1 22.1 us: supply_steps_all(): lax.psum(slab_in, axis_name=peer_axis)]
    dot_general x9, matrix products: 4.37 us -> 10.7 us  [kernel_terms(): lax.dot_general(window, flat_slopes, (((0,), (0,)), ((), ())), preferred_...]
    dot_general x9, matrix products: 6.51 us -> 11.7 us  [conv_adjoint(): lax.dot_general(window, kernel[row_off, col_off], (((1,), (1,)), ((), ())...]
    unnamed x25 -> x31, local copies, waits for them, and re-layouts: 6.52 us -> 8.51 us
  transfers between devices with their start and end apart: 6 -> 7, of which waited for: 4 -> 5; matrix products, arithmetic and copies ran while one was open for 7% -> 11% of each run, Pallas kernels for 0% -> 0%
where the time goes in v1:
time: 318 us; the launch traced here: 317 us
  waiting for transfers between devices  156 us (49%)
  blocking collectives  57.3 us (18%)
  other arithmetic  28.7 us (9%)
  matrix products  27.5 us (9%)
  between operations  17.4 us (5%)
  starting transfers between devices  15.6 us (5%)
  local copies, waits for them, and re-layouts  14.1 us (4%)
    psum x1, waiting for transfers between devices, supply_steps_all(): lax.psum(slab_in, axis_name=peer_axis)  82.6 us
    psum x1, waiting for transfers between devices, supply_steps_all(): lax.psum(lax.psum(slab_in, axis_name=peer_axis), axis_name=shard_axis)  51.5 us
    all_to_all x1, blocking collectives, local(): lax.all_to_all(fields, 'ens', split_axis=1, concat_axis=0, tiled=True)  28.3 us
    psum x1, blocking collectives, supply_steps_all(): lax.psum(slab_in, axis_name=peer_axis)  22.1 us
    all_to_all x1, waiting for transfers between devices, local(): lax.all_to_all(slope, 'ens', split_axis=0, concat_axis=1, tiled=True)  21.1 us
    dot_general x9, matrix products, conv_adjoint(): lax.dot_general(window, kernel[row_off, col_off], (((1,), (1,)), ((), ())...  11.7 us
    dot_general x9, matrix products, kernel_terms(): lax.dot_general(window, flat_slopes, (((0,), (0,)), ((), ())), preferred_...  10.7 us
    reduce_sum x1, other arithmetic, local(): slope = jnp.sum(gap / width, axis=1)  9.94 us
  transfers between devices with their start and end apart: 7, of which 5 were waited for; matrix products, arithmetic and copies ran while one was open for 11% of the time, Pallas kernels for 0%

profile of v1, /device:TPU:0, one launch (start us, length us, event | category | flops | bytes accessed | tf_op | source)
XLA Modules:
  0.0 316.7 jit_solution(5856451937051660011)
XLA Ops:
  7.2 1.2 fusion.72
  8.4 3.0 collective-permute-start
  11.4 3.1 collective-permute-start.1
  14.5 1.7 fusion.33
  16.2 0.6 collective-permute-done
  16.8 0.3 collective-permute-done.1
  17.1 0.8 select_maximum_fusion.2
  17.9 1.0 fusion.70
  18.9 0.3 copy-done.9
  19.2 0.4 fusion.27
  19.6 0.4 fusion.43
  20.1 0.4 convolution_add_fusion.11
  20.5 0.4 convolution_add_fusion.10
  20.9 1.2 pad_maximum_fusion.2
  22.2 0.4 fusion.8
  22.6 0.5 copy-done.5
  23.1 0.4 copy-done.3
  23.5 0.4 fusion.7
  23.9 0.4 convolution_add_fusion.7
  24.3 0.4 convolution_add_fusion.6
  24.9 28.3 %all_to_all.24 = f32[2,32,32,256]{3,2,0,1:T(8,128)S(1)} all-to-all(f32[2,32,32,256]{3,2,0,1:T(8,128)S(1)} %copy.19), channel_id=1, replica_groups=mesh['ens'=4,'space'=8] {'ens'}, dimensions={1} | all-to-all | bytes 4194304 | tf_op jit(solution)/shard_map/all_to_all | solution.py:98
  53.2 0.2 copy.21
  53.4 9.9 %fusion.3 = (f32[8,8,32,256]{3,2,1,0:T(8,128)}, f32[8,32,256]{2,1,0:T(8,128)}) fusion(f32[8,8,32,256]{3,2,1,0:T(8,128)S(1)} %bitcast.208), kind=kLoop, calls=%fused_computation.5 | loop fusion | flops 24576000 | bytes 4456448 | tf_op jit(solution)/shard_map/reduce_sum | solution.py:101
  63.4 4.4 %all-to-all-start.1 = ((f32[8,8,32,256]{3,2,1,0:T(8,128)}), f32[8,8,32,256]{3,2,1,0:T(8,128)}, u32[]{:S(2)}, u32[]{:S(2)}) async-start(f32[8,8,32,256]{3,2,1,0:T(8,128)} %get-tuple-element.3), calls=%async_computation.1 | async-start | bytes 4194304 | tf_op jit(solution)/shard_map/all_to_all | solution.py:102
  68.1 2.1 convert_element_type.18
  70.2 1.6 add_reduce_fusion
  72.5 21.1 %all-to-all-done.1 = f32[8,8,32,256]{3,2,1,0:T(8,128)} async-done(((f32[8,8,32,256]{3,2,1,0:T(8,128)}), f32[8,8,32,256]{3,2,1,0:T(8,128)}, u32[]{:S(2)}, u32[]{:S(2)}) %all-to-all-start.1) | async-done | bytes 2097184 | tf_op jit(solution)/shard_map/all_to_all | solution.py:102
  93.6 1.8 broadcast_multiply_fusion.1
  95.4 0.2 copy.22
  95.7 1.0 copy-done.7
  96.6 2.8 fusion.10
  99.4 2.3 subtract_convert_fusion
  101.6 1.2 fusion.20
  103.6 22.1 %psum.28 = f32[]{:T(128)} all-reduce(f32[]{:T(128)S(6)} %sub.50), channel_id=1, replica_groups=mesh['ens'=4,'space'=8] {'space'}, use_global_device_ids=true, to_apply=%region_3.4 | all-reduce | flops 1 | bytes 8 | tf_op jit(solution)/shard_map/psum | solution.py:11
  125.7 4.7 %collective-permute-start.3 = (bf16[2,32,1,256]{3,2,1,0:T(2,128)(2,1)S(1)}, bf16[2,32,1,256]{3,2,1,0:T(2,128)(2,1)S(1)}, u32[]{:S(2)}, u32[]{:S(2)}) collective-permute-start(bf16[2,32,1,256]{3,2,1,0:T(2,128)(2,1)S(1)} %get-tuple-element.22), channel_id=1, source_target_pairs={{1,0},{2,1},{3,2},{4,3},{5,4},{6,5},{7,6},{0,7},{9,8},{10,9},{11,1... | collective-permute-start | bytes 98312 | tf_op jit(solution)/shard_map/ppermute | solution.py:27
  130.4 1.2 fusion.19
  131.6 1.2 fusion.18
  132.9 1.2 fusion.17
  134.0 1.2 fusion.16
  135.3 1.2 fusion.15
  136.4 1.2 fusion.14
  137.6 1.2 fusion.13
  138.8 1.2 fusion.12
  140.0 3.3 %broadcast_multiply_fusion = f32[9,256,256]{2,1,0:T(8,128)} fusion(f32[9,256,256]{2,1,0:T(8,128)} %fusion.12), kind=kLoop, calls=%fused_computation.37 | loop fusion | flops 589824 | bytes 4718592 | tf_op jit(solution)/shard_map/div | solution.py:109
  143.3 1.1 copy-done.11
  144.5 2.7 fusion.31
  147.2 6.9 %psum.29 = f32[]{:T(128)} all-reduce(f32[]{:T(128)} %psum.28), channel_id=1, replica_groups=mesh['ens'=4,'space'=8] {'ens'}, use_global_device_ids=true, to_apply=%region_4.5 | all-reduce | flops 1 | bytes 8 | tf_op jit(solution)/shard_map/psum | solution.py:11
  154.8 2.1 pad_maximum_fusion
  156.9 0.8 select_maximum_fusion
  157.7 2.7 fusion.69
  160.4 1.4 fusion.41
  161.7 1.4 convolution_add_fusion.5
  163.1 1.5 convolution_add_fusion.4
  164.8 0.3 copy-done.10
  165.1 0.5 fusion.6
  165.7 82.6 %all-reduce.5.cloned.1.call-done = f32[3,3,256,256]{3,2,1,0:T(8,128)} async-done(((f32[3,3,256,256]{3,2,1,0:T(8,128)}), f32[3,3,256,256]{3,2,1,0:T(8,128)}) %all-reduce.5.cloned.1.call-update) | async-done | bytes 2359312 | tf_op jit(solution)/shard_map/psum | solution.py:11
  248.4 1.8 fusion.25
  250.2 0.5 fusion.5
  250.6 0.7 copy-done.14
  251.4 0.5 convolution_add_fusion.1
  251.9 0.7 copy-done.13
  252.6 1.4 fusion.9
  254.0 51.5 %all-reduce.7.cloned.1.call-done = f32[3,3,256,256]{3,2,1,0:T(8,128)} async-done(((f32[3,3,256,256]{3,2,1,0:T(8,128)}), f32[3,3,256,256]{3,2,1,0:T(8,128)}) %all-reduce.7.cloned.1.call-update) | async-done | bytes 2359312 | tf_op jit(solution)/shard_map/psum | solution.py:11
  305.5 3.2 %copy.46 = f32[3,3,256,256]{3,2,1,0:T(8,128)} copy(f32[3,3,256,256]{3,2,1,0:T(8,128)} %all-reduce.7.cloned.1.call-done) | data formatting | bytes 4718592
  (31 shorter events, 0.8 us)
Async XLA Ops:
  7.2 9.9 %copy-start.1 = (bf16[2,32,32,256]{3,2,1,0:T(8,128)(2,1)S(1)}, bf16[2,32,32,256]{3,2,1,0:T(8,128)(2,1)}, u32[]{:S(2)}) copy-start(bf16[2,32,32,256]{3,2,1,0:T(8,128)(2,1)} %param.3) | copy-start | bytes 3145732
  8.4 8.4 %collective-permute-start = (bf16[2,32,1,256]{3,2,1,0:T(2,128)(2,1)S(1)}, bf16[2,32,1,256]{3,2,1,0:T(2,128)(2,1)S(1)}, u32[]{:S(2)}, u32[]{:S(2)}) collective-permute-start(bf16[2,32,1,256]{3,2,1,0:T(2,128)(2,1)S(1)} %get-tuple-element.25), channel_id=1, source_target_pairs={{0,1},{1,2},{2,3},{3,4},{4,5},{5,6},{6,7},{7,0},{8,9},{9,10},{10,1... | collective-permute-start | bytes 98312 | tf_op jit(solution)/shard_map/ppermute | solution.py:24
  11.4 5.7 %collective-permute-start.1 = (bf16[2,32,1,256]{3,2,1,0:T(2,128)(2,1)S(1)}, bf16[2,32,1,256]{3,2,1,0:T(2,128)(2,1)S(1)}, u32[]{:S(2)}, u32[]{:S(2)}) collective-permute-start(bf16[2,32,1,256]{3,2,1,0:T(2,128)(2,1)S(1)} %get-tuple-element.26), channel_id=1, source_target_pairs={{1,0},{2,1},{3,2},{4,3},{5,4},{6,5},{7,6},{0,7},{9,8},{10,9},{11,1... | collective-permute-start | bytes 98312 | tf_op jit(solution)/shard_map/ppermute | solution.py:27
  17.9 1.3 copy-start.9
  22.1 1.0 copy-start.5
  22.2 1.3 copy-start.3
  24.8 70.9 %copy-start = (f32[2048,256]{1,0:T(8,128)}, f32[2048,256]{1,0:T(8,128)S(1)}, u32[]{:S(2)}) copy-start(f32[2048,256]{1,0:T(8,128)S(1)} %convolution_add_fusion.6) | copy-start | bytes 6291460
  63.4 30.2 %all-to-all-start.1 = ((f32[8,8,32,256]{3,2,1,0:T(8,128)}), f32[8,8,32,256]{3,2,1,0:T(8,128)}, u32[]{:S(2)}, u32[]{:S(2)}) async-start(f32[8,8,32,256]{3,2,1,0:T(8,128)} %get-tuple-element.3), calls=%async_computation.1 | async-start | bytes 4194304 | tf_op jit(solution)/shard_map/all_to_all | solution.py:102
  67.8 180.5 %all-reduce.5.cloned.1.call-start = ((), (), s32[]{:S(2)}) async-start(), calls=%async_computation.2 | async-start | bytes 4718592 | tf_op jit(solution)/shard_map/psum | solution.py:11
  95.4 1.2 copy-start.7
  125.7 29.0 %collective-permute-start.2 = (bf16[2,32,1,256]{3,2,1,0:T(2,128)(2,1)S(1)}, bf16[2,32,1,256]{3,2,1,0:T(2,128)(2,1)S(1)}, u32[]{:S(2)}, u32[]{:S(2)}) collective-permute-start(bf16[2,32,1,256]{3,2,1,0:T(2,128)(2,1)S(1)} %get-tuple-element.21), channel_id=1, source_target_pairs={{0,1},{1,2},{2,3},{3,4},{4,5},{5,6},{6,7},{7,0},{8,9},{9,10},{10,1... | collective-permute-start | bytes 98312 | tf_op jit(solution)/shard_map/ppermute | solution.py:24
  125.7 29.0 %collective-permute-start.3 = (bf16[2,32,1,256]{3,2,1,0:T(2,128)(2,1)S(1)}, bf16[2,32,1,256]{3,2,1,0:T(2,128)(2,1)S(1)}, u32[]{:S(2)}, u32[]{:S(2)}) collective-permute-start(bf16[2,32,1,256]{3,2,1,0:T(2,128)(2,1)S(1)} %get-tuple-element.22), channel_id=1, source_target_pairs={{1,0},{2,1},{3,2},{4,3},{5,4},{6,5},{7,6},{0,7},{9,8},{10,9},{11,1... | collective-permute-start | bytes 98312 | tf_op jit(solution)/shard_map/ppermute | solution.py:27
  131.6 1.2 copy-start.6
  131.6 2.4 copy-start.2
  132.9 2.4 copy-start.4
  143.3 1.2 copy-start.11
  143.3 162.3 %all-reduce.7.cloned.1.call-start = ((), (), s32[]{:S(2)}) async-start(), calls=%async_computation.3 | async-start | bytes 4718592 | tf_op jit(solution)/shard_map/psum | solution.py:11
  163.1 1.7 copy-start.8
  163.1 2.0 copy-start.10
  248.3 1.8 copy-start.12
  250.1 1.2 copy-start.14
  251.4 1.2 copy-start.13
Sparse Core Ops, SparseCore 0:
  143.4 104.8 all-reduce.4
  250.8 54.6 all-reduce.6
